TPU v7x, 256 devices: a whole 4x4x8 slice. The times are simulated.
256 devices in a mesh: tm: 8 (over z), seq: 32 (over y, x, core).
Axes of the slice: x: 4, y: 4, z: 8, core: 2. Of those that a mesh axis runs over, the one named last changes fastest.
Arguments:
- states: float32 [64, 1536, 64], P('tm', 'seq'), may hold values from -11 to 11
- first_state: float32 [1536, 64], P('seq'), may hold values from -6 to 6
- now_step: int32 [64], P('tm'), may hold values from 1 to 960, as said below
- next_step: int32 [64], P('tm'), may hold values from 0 to 959, as said below
- embed_weight: bfloat16 [64, 1536], replicated, may hold values from -0.75 to 0.75
- mod_weight: bfloat16 [256, 4608], replicated, may hold values from -0.375 to 0.375
- qkv_weight: bfloat16 [1536, 12, 384], P('seq'), may hold values from -1 to 1
- out_weight: bfloat16 [1536, 1536], P('seq'), may hold values from -0.15625 to 0.15625
- final_weight: bfloat16 [1536, 64], replicated, may hold values from -0.15625 to 0.15625
Outputs:
- advanced: float32 [64, 1536, 64], P('tm', 'seq')
- errors: float32 [64], P('tm')
Inputs may be any that keep to these rules, and one draw needn't show every extreme that they name: now_step[0] = 960 and now_step[j + 1] = next_step[j]. next_step[j] is now_step[j] minus a gap of 1 to 15.
All inputs are finite; a program needn't handle non-finite values.
Results may differ from a plain program's by a relative error of at most 0.002.
Values may be sent and summed in bfloat16 or wider, within the bound.
A program may use at most 64 MiB of HBM per device.

v0:
```python
import math
import jax
import jax.numpy as jnp
from jax import lax
from jax.sharding import PartitionSpec as P


def from_behind(shard, axis, by):
    count = lax.axis_size(axis)
    pairs = [(i, i + by) for i in range(count) if 0 <= i + by < count]
    return lax.ppermute(shard, axis, pairs)


def entering(part, axis, combine, identity):
    place = lax.axis_index(axis)
    gathered = lax.all_gather(part, axis)
    state = jnp.zeros_like(part) + jnp.asarray(identity, part.dtype)

    def one(step, state):
        return combine(state, lax.dynamic_index_in_dim(gathered, step, 0, False))

    return lax.fori_loop(0, place, one, state)


def layer_norm(rows):
    row_mean = jnp.mean(rows, axis=-1, keepdims=True)
    centered = rows - row_mean
    variance = jnp.mean(centered * centered, axis=-1, keepdims=True)
    return centered * lax.rsqrt(variance + 1e-06)


def alpha_bar(step_ids):
    fraction = (step_ids.astype(jnp.float32) / 1000.0 + 0.008) / 1.008
    return jnp.cos(fraction * (math.pi / 2)) ** 2


def coefficients(now_step, next_step):
    alpha_now = alpha_bar(now_step)
    alpha_next = alpha_bar(next_step)
    step_ratio = jnp.sqrt(alpha_next / alpha_now)
    keep_coef = step_ratio - 1.0
    noise_coef = jnp.sqrt(1.0 - alpha_next) - step_ratio * jnp.sqrt(1.0 - alpha_now)
    return (keep_coef, noise_coef)


def modulation(step_ids, mod_weight):
    half_freq = mod_weight.shape[0] // 2
    frequency = jnp.exp(-math.log(10000.0) * jnp.arange(half_freq, dtype=jnp.float32) / half_freq)
    angles = step_ids.astype(jnp.float32)[:, None] * frequency[None, :]
    time_embed = jnp.concatenate([jnp.cos(angles), jnp.sin(angles)], axis=1).astype(jnp.bfloat16)
    return jnp.dot(time_embed, mod_weight, preferred_element_type=jnp.float32)


def attend_one(pair_item):
    hdim = pair_item.shape[1] // 3
    length = pair_item.shape[0]
    query_rows = 512
    queries = pair_item[:, :hdim]
    key_rows = pair_item[:, hdim : 2 * hdim]
    values = pair_item[:, 2 * hdim :]

    def one_block(query_block):
        scores = jnp.dot(query_block, key_rows.T, preferred_element_type=jnp.float32) * hdim ** (
            -0.5
        )
        row_max = jnp.max(scores, axis=1, keepdims=True)
        exponent = jnp.exp(scores - row_max)
        weights = (exponent / jnp.sum(exponent, axis=1, keepdims=True)).astype(jnp.bfloat16)
        return jnp.dot(weights, values, preferred_element_type=jnp.float32).astype(jnp.bfloat16)

    blocks_out = lax.map(one_block, queries.reshape(length // query_rows, query_rows, hdim))
    return blocks_out.reshape(length, hdim)


def attend_pairs(pair_block):
    return lax.map(attend_one, pair_block[0])[None]


def add_terms(earlier, later):
    return earlier + later


def per_device(
    states,
    first_state,
    now_step,
    next_step,
    embed_weight,
    mod_weight,
    qkv_weight,
    out_weight,
    final_weight,
):
    step_count, tokd, chans = states.shape
    seq_devs = lax.axis_size("seq")
    time_index = lax.axis_index("tm")
    heads = qkv_weight.shape[1]
    width_three = qkv_weight.shape[2]
    hdim = width_three // 3
    width = heads * hdim
    edge_state = from_behind(states[-1], "tm", 1)
    opening = jnp.where(time_index == 0, first_state, edge_state)
    previous = jnp.concatenate([opening[None], states[:-1]], axis=0)
    keep_coef, noise_coef = coefficients(now_step, next_step)
    modulated_all = modulation(now_step, mod_weight)
    shift_mod = modulated_all[:, :width]
    scale_mod = modulated_all[:, width : 2 * width]
    gate_mod = modulated_all[:, 2 * width :]
    residual = jnp.einsum(
        "tsc,cd->tsd",
        previous.astype(jnp.bfloat16),
        embed_weight,
        preferred_element_type=jnp.float32,
    )
    modulated = (
        layer_norm(residual) * (1.0 + scale_mod[:, None, :]) + shift_mod[:, None, :]
    ).astype(jnp.bfloat16)
    columns = modulated
    projected = jnp.einsum(
        "tsd,dhc->thsc",
        columns,
        lax.all_gather(qkv_weight, "seq", axis=0, tiled=True),
        preferred_element_type=jnp.float32,
    ).astype(jnp.bfloat16)
    pair_count = step_count * heads
    per_dev = pair_count // seq_devs
    grouped = projected.reshape(seq_devs, per_dev, tokd, width_three)
    routed = attend_pairs(lax.all_to_all(grouped, "seq", split_axis=0, concat_axis=2, tiled=True))
    returned = lax.all_to_all(routed, "seq", split_axis=2, concat_axis=0, tiled=True)
    flattened = jnp.transpose(
        returned.reshape(step_count, heads, tokd, hdim), (0, 2, 1, 3)
    ).reshape(step_count, tokd, width)
    columns = flattened
    projection = jnp.einsum(
        "tsd,de->tse",
        columns,
        lax.all_gather(out_weight, "seq", axis=0, tiled=True),
        preferred_element_type=jnp.float32,
    )
    updated = residual + gate_mod[:, None, :] * projection
    normed_out = layer_norm(updated).astype(jnp.bfloat16)
    noise_pred = jnp.einsum(
        "tsd,dc->tsc", normed_out, final_weight, preferred_element_type=jnp.float32
    )
    drift_terms = keep_coef[:, None, None] * previous + noise_coef[:, None, None] * noise_pred
    running_sums = jnp.cumsum(drift_terms, axis=0)
    block_total = running_sums[-1]
    carried = entering(block_total, "tm", add_terms, jnp.zeros_like(block_total))
    advanced = first_state[None] + carried[None] + running_sums
    difference = advanced - states
    partial_value = jnp.sum(difference * difference, axis=(1, 2))
    errors = lax.psum(partial_value, "seq") / (tokd * seq_devs * chans)
    return (advanced, errors)


def solution(mesh):
    in_specs = (
        P("tm", "seq", None),
        P("seq", None),
        P("tm"),
        P("tm"),
        P(),
        P(),
        P("seq", None, None),
        P("seq", None),
        P(),
    )
    out_specs = (P("tm", "seq", None), P("tm"))
    return jax.shard_map(
        per_device, mesh=mesh, in_specs=in_specs, out_specs=out_specs, check_vma=False
    )
```

profile of v0, /device:TPU:1, one launch (start us, length us, event | category | flops | bytes accessed | tf_op | source)
XLA Modules:
  0.0 330.8 jit_solution(13507943861712329472)
XLA Ops:
  8.8 4.3 %collective-permute-start = (f32[48,64]{1,0:T(8,128)S(1)}, f32[48,64]{1,0:T(8,128)S(1)}, u32[]{:S(2)}, u32[]{:S(2)}) collective-permute-start(f32[48,64]{1,0:T(8,128)S(1)} %slice_bitcast_fusion), channel_id=1, source_target_pairs={{0,32},{32,64},{64,96},{96,128},{128,160},{160,192},{192,224},{1,3... | collective-permute-start | bytes 36872 | tf_op jit(solution)/shard_map/ppermute | solution.py:11
  16.2 1.4 copy-done.1
  18.0 68.3 %all-gather.3.cloned.1.call-done = bf16[1536,12,384]{2,0,1:T(8,128)(2,1)} async-done(((bf16[48,12,384]{2,0,1:T(8,128)(2,1)}), bf16[1536,12,384]{2,0,1:T(8,128)(2,1)}) %all-gather.3.cloned.1.call-update) | async-done | bytes 14155792 | tf_op jit(solution)/shard_map/all_gather | solution.py:122
  86.3 11.1 %fusion.18 = bf16[8,48,12,384]{3,1,2,0:T(8,128)(2,1)} fusion(bf16[1536,12,384]{2,0,1:T(8,128)(2,1)} %all-gather.3.cloned.1.call-done, f32[8,48,1536]{2,1,0:T(8,128)} %copy-done.1, f32[8,1536]{1,0:T(8,128)S(1)} %get-tuple-element.105, f32[8,1536]{1,0:T(8,128)S(1)} %get-tuple-element.106, f32[8,48]{1,0:T(8,128)S(1)} %add_rsqrt_fusion.1, ...), kind=kOutput, calls=%fused_computation.20 | convolution fusion | flops 5440536576 | bytes 20155392 | tf_op jit(solution)/shard_map/tsd,dhc->thsc/dot_general | solution.py:119
  97.3 5.5 %all-to-all-start = ((bf16[32,3,48,384]{3,2,1,0:T(8,128)(2,1)}), bf16[32,3,48,384]{3,2,1,0:T(8,128)(2,1)}, u32[]{:S(2)}, u32[]{:S(2)}) async-start(bf16[32,3,48,384]{3,2,1,0:T(8,128)(2,1)} %bitcast.93), calls=%async_computation | async-start | bytes 7077888 | tf_op jit(solution)/shard_map/all_to_all | solution.py:128
  103.6 44.9 %all-to-all-done = bf16[32,3,48,384]{3,2,1,0:T(8,128)(2,1)} async-done(((bf16[32,3,48,384]{3,2,1,0:T(8,128)(2,1)}), bf16[32,3,48,384]{3,2,1,0:T(8,128)(2,1)}, u32[]{:S(2)}, u32[]{:S(2)}) %all-to-all-start) | async-done | bytes 3538976 | tf_op jit(solution)/shard_map/all_to_all | solution.py:128
  148.5 4.1 %copy.17 = bf16[1,3,32,48,384]{4,3,2,1,0:T(8,128)(2,1)} copy(bf16[1,3,32,48,384]{4,3,1,2,0:T(8,128)(2,1)} %bitcast.15) | data formatting | bytes 7077888 | tf_op jit(solution)/shard_map/all_to_all | solution.py:128
  152.6 33.7 %while.31 = (s32[]{:T(128)}, bf16[3,1536,128]{2,1,0:T(8,128)(2,1)}, bf16[3,1536,384]{2,1,0:T(8,128)(2,1)}, s32[]{:T(128)}, s32[]{:T(128)}, /*index=5*/s32[]{:T(128)}) while((s32[]{:T(128)}, bf16[3,1536,128]{2,1,0:T(8,128)(2,1)}, bf16[3,1536,384]{2,1,0:T(8,128)(2,1)}, s32[]{:T(128)}, s32[]{:T(128)}, /*index=5*/s32[]{:T(128)}) %tuple.79), condition=%wide.region_7.8_spmd, body=%wide.region_2.7_spmd.sunk | while | flops 408222720 | bytes 16002250 | solution.py:76
  152.6 1.4 dynamic-slice_bitcast_fusion.2
  154.2 7.8 %while.33 = (s32[]{:T(128)}, bf16[3,512,128]{2,1,0:T(8,128)(2,1)}, bf16[3,512,128]{2,1,0:T(8,128)(2,1)S(1)}, bf16[1536,128]{1,0:T(8,128)(2,1)S(1)}, bf16[1536,128]{1,0:T(8,128)(2,1)S(1)}, /*index=5*/s32[]{:T(128)}) while((s32[]{:T(128)}, bf16[3,512,128]{2,1,0:T(8,128)(2,1)}, bf16[3,512,128]{2,1,0:T(8,128)(2,1)S(1)}, ...), condition=%wide.region_6.6_spmd, body=%wide.region_3.5_spmd.sunk | while | flops 408222720 | bytes 10496585 | solution.py:71
  158.1 1.4 fusion.70
  160.7 1.4 fusion.70
  162.1 1.8 bitcast_dynamic-update-slice_fusion.2
  163.8 1.4 dynamic-slice_bitcast_fusion.2
  165.5 7.8 %while.33 = (s32[]{:T(128)}, bf16[3,512,128]{2,1,0:T(8,128)(2,1)}, bf16[3,512,128]{2,1,0:T(8,128)(2,1)S(1)}, bf16[1536,128]{1,0:T(8,128)(2,1)S(1)}, bf16[1536,128]{1,0:T(8,128)(2,1)S(1)}, /*index=5*/s32[]{:T(128)}) while((s32[]{:T(128)}, bf16[3,512,128]{2,1,0:T(8,128)(2,1)}, bf16[3,512,128]{2,1,0:T(8,128)(2,1)S(1)}, ...), condition=%wide.region_6.6_spmd, body=%wide.region_3.5_spmd.sunk | while | flops 408222720 | bytes 10496585 | solution.py:71
  166.7 1.4 fusion.70
  169.3 1.4 fusion.70
  171.9 1.4 fusion.70
  173.3 1.8 bitcast_dynamic-update-slice_fusion.2
  175.1 1.4 dynamic-slice_bitcast_fusion.2
  176.7 7.8 %while.33 = (s32[]{:T(128)}, bf16[3,512,128]{2,1,0:T(8,128)(2,1)}, bf16[3,512,128]{2,1,0:T(8,128)(2,1)S(1)}, bf16[1536,128]{1,0:T(8,128)(2,1)S(1)}, bf16[1536,128]{1,0:T(8,128)(2,1)S(1)}, /*index=5*/s32[]{:T(128)}) while((s32[]{:T(128)}, bf16[3,512,128]{2,1,0:T(8,128)(2,1)}, bf16[3,512,128]{2,1,0:T(8,128)(2,1)S(1)}, ...), condition=%wide.region_6.6_spmd, body=%wide.region_3.5_spmd.sunk | while | flops 408222720 | bytes 10496585 | solution.py:71
  177.9 1.4 fusion.70
  180.6 1.4 fusion.70
  183.2 1.4 fusion.70
  184.6 1.8 bitcast_dynamic-update-slice_fusion.2
  186.3 8.1 %copy.31 = bf16[3,1536,128]{2,0,1:T(4,128)(2,1)} copy(bf16[3,1536,128]{2,1,0:T(8,128)(2,1)} %get-tuple-element.69) | data formatting | bytes 2359296 | tf_op jit(solution)/shard_map/while | solution.py:76
  194.4 7.4 %all-to-all-start.1 = ((bf16[1,3,1536,128]{3,1,0,2:T(4,128)(2,1)}), bf16[1,3,1536,128]{3,1,0,2:T(4,128)(2,1)}, u32[]{:S(2)}, u32[]{:S(2)}) async-start(bf16[1,3,1536,128]{3,1,0,2:T(4,128)(2,1)} %bitcast.91), calls=%async_computation.1 | async-start | bytes 3145728 | tf_op jit(solution)/shard_map/all_to_all | solution.py:129
  202.0 22.2 %all-to-all-done.1 = bf16[1,3,1536,128]{3,1,0,2:T(4,128)(2,1)} async-done(((bf16[1,3,1536,128]{3,1,0,2:T(4,128)(2,1)}), bf16[1,3,1536,128]{3,1,0,2:T(4,128)(2,1)}, u32[]{:S(2)}, u32[]{:S(2)}) %all-to-all-start.1) | async-done | bytes 1179680 | tf_op jit(solution)/shard_map/all_to_all | solution.py:129
  224.2 1.6 copy.19
  225.9 5.1 %fusion.55 = (f32[8,48]{1,0:T(8,128)S(1)}, f32[8,48,1536]{2,1,0:T(8,128)S(1)}) fusion(f32[8,48,1536]{2,1,0:T(8,128)} %copy-done.1, bf16[1536,1536]{1,0:T(8,128)(2,1)} %all-gather.5.cloned.1.call-done, bf16[8,12,6,8,128]{4,3,2,1,0:T(8,128)(2,1)S(1)} %bitcast.94, f32[8,1536]{1,0:T(8,128)} %get-tuple-element.104), kind=kOutput, calls=%fused_computation.77 | convolution fusion | flops 1813708416 | bytes 10667520 | tf_op jit(solution)/shard_map/tsd,de->tse/dot_general | solution.py:134
  232.6 20.1 %all_gather.11 = f32[8,48,64]{2,1,0:T(8,128)S(1)} all-gather(f32[1,48,64]{2,1,0:T(8,128)S(1)} %slice.39), channel_id=1, replica_groups=mesh['tm'=8,'seq'=32] {'tm'}, dimensions={0}, use_global_device_ids=true | all-gather | bytes 110592 | tf_op jit(solution)/shard_map/all_gather | solution.py:16
  253.5 70.0 %psum.7 = f32[8]{0:T(128)S(1)} all-reduce(f32[8]{0:T(128)S(1)} %get-tuple-element.95), channel_id=1, replica_groups=mesh['tm'=8,'seq'=32] {'seq'}, use_global_device_ids=true, to_apply=%region_14.15 | all-reduce | flops 8 | bytes 64 | tf_op jit(solution)/shard_map/psum | solution.py:152
  (85 shorter events, 21.7 us)
Async XLA Ops:
  7.2 6.7 %copy-start = (bf16[256,4608]{1,0:T(8,128)(2,1)S(1)}, bf16[256,4608]{1,0:T(8,128)(2,1)}, u32[]{:S(2)}) copy-start(bf16[256,4608]{1,0:T(8,128)(2,1)} %param.20) | copy-start | bytes 7077892
  7.2 7.8 %copy-start.4 = (f32[8,48,64]{2,1,0:T(8,128)S(1)}, f32[8,48,64]{2,1,0:T(8,128)}, u32[]{:S(2)}) copy-start(f32[8,48,64]{2,1,0:T(8,128)} %param.15) | copy-start | bytes 294916
  7.2 7.8 %copy-start.10 = (f32[48,64]{1,0:T(8,128)S(1)}, f32[48,64]{1,0:T(8,128)}, u32[]{:S(2)}) copy-start(f32[48,64]{1,0:T(8,128)} %param.16) | copy-start | bytes 36868
  7.2 8.4 %copy-start.9 = (bf16[64,1536]{1,0:T(8,128)(2,1)S(1)}, bf16[64,1536]{1,0:T(8,128)(2,1)}, u32[]{:S(2)}) copy-start(bf16[64,1536]{1,0:T(8,128)(2,1)} %param.19) | copy-start | bytes 589828
  7.2 79.0 %all-gather.3.cloned.1.call-start = ((), (), s32[]{:S(2)}) async-start(), calls=%async_computation.2 | async-start | bytes 14598144 | tf_op jit(solution)/shard_map/all_gather | solution.py:122
  8.8 6.2 %collective-permute-start = (f32[48,64]{1,0:T(8,128)S(1)}, f32[48,64]{1,0:T(8,128)S(1)}, u32[]{:S(2)}, u32[]{:S(2)}) collective-permute-start(f32[48,64]{1,0:T(8,128)S(1)} %slice_bitcast_fusion), channel_id=1, source_target_pairs={{0,32},{32,64},{64,96},{96,128},{128,160},{160,192},{192,224},{1,3... | collective-permute-start | bytes 36872 | tf_op jit(solution)/shard_map/ppermute | solution.py:11
  15.0 3.0 copy-start.2
  15.0 0.6 copy-start.6
  16.2 1.4 copy-start.1
  97.3 51.2 %all-to-all-start = ((bf16[32,3,48,384]{3,2,1,0:T(8,128)(2,1)}), bf16[32,3,48,384]{3,2,1,0:T(8,128)(2,1)}, u32[]{:S(2)}, u32[]{:S(2)}) async-start(bf16[32,3,48,384]{3,2,1,0:T(8,128)(2,1)} %bitcast.93), calls=%async_computation | async-start | bytes 7077888 | tf_op jit(solution)/shard_map/all_to_all | solution.py:128
  102.8 123.1 %all-gather.5.cloned.1.call-start = ((), (), s32[]{:S(2)}) async-start(), calls=%async_computation.3 | async-start | bytes 4866048 | tf_op jit(solution)/shard_map/all_gather | solution.py:137
  186.3 15.5 %copy-start.12 = (s32[8]{0:T(128)S(1)}, s32[8]{0:T(128)}, u32[]{:S(2)}) copy-start(s32[8]{0:T(128)} %param.17) | copy-start | bytes 100
  186.3 15.5 %copy-start.13 = (s32[8]{0:T(128)S(1)}, s32[8]{0:T(128)}, u32[]{:S(2)}) copy-start(s32[8]{0:T(128)} %param.18) | copy-start | bytes 100
  194.4 29.8 %all-to-all-start.1 = ((bf16[1,3,1536,128]{3,1,0,2:T(4,128)(2,1)}), bf16[1,3,1536,128]{3,1,0,2:T(4,128)(2,1)}, u32[]{:S(2)}, u32[]{:S(2)}) async-start(bf16[1,3,1536,128]{3,1,0,2:T(4,128)(2,1)} %bitcast.91), calls=%async_computation.1 | async-start | bytes 3145728 | tf_op jit(solution)/shard_map/all_to_all | solution.py:129
  231.0 0.9 copy-start.8
  231.1 1.5 copy-start.3
  231.1 1.4 copy-start.7
  231.5 21.3 %copy-start.11 = (f32[48,64]{1,0:T(8,128)S(1)}, f32[48,64]{1,0:T(8,128)}, u32[]{:S(2)}) copy-start(f32[48,64]{1,0:T(8,128)} %param.16) | copy-start | bytes 36868
  231.5 21.3 %copy-start.5 = (f32[8,48,64]{2,1,0:T(8,128)S(1)}, f32[8,48,64]{2,1,0:T(8,128)}, u32[]{:S(2)}) copy-start(f32[8,48,64]{2,1,0:T(8,128)} %param.15) | copy-start | bytes 294916
Sparse Core Ops, SparseCore 0:
  10.7 75.5 all-gather.2
  106.2 68.7 all-gather.4
where the time goes:
time: 331 us
  waiting for transfers between devices  137 us (41%)
  blocking collectives  90.1 us (27%)
  matrix products  36 us (11%)
  local copies, waits for them, and re-layouts  27.4 us (8%)
  starting transfers between devices  17.3 us (5%)
  between operations  14.4 us (4%)
  other arithmetic  8.79 us (3%)
    psum x1, blocking collectives, per_device(): errors = lax.psum(partial_value, 'seq') / (tokd * seq_devs * chans)  70 us
    all_gather x1, waiting for transfers between devices, per_device(): lax.all_gather(qkv_weight, 'seq', axis=0, tiled=True)  68.3 us
    all_to_all x1, waiting for transfers between devices, per_device(): lax.all_to_all(grouped, 'seq', split_axis=0, concat_axis=2, tiled=True)  44.9 us
    all_to_all x1, waiting for transfers between devices, per_device(): lax.all_to_all(routed, 'seq', split_axis=2, concat_axis=0, tiled=True)  22.2 us
    all_gather x1, blocking collectives, entering(): gathered = lax.all_gather(part, axis)  20.1 us
    dot_general x9, matrix products, one_block(): jnp.dot(weights, values, preferred_element_type=jnp.float32)  12.4 us
    dot_general x1, matrix products, per_device(): jnp.einsum('tsd,dhc->thsc', columns, lax.all_gather(qkv_weight, 'seq', ax...  11.1 us
    while x1, local copies, waits for them, and re-layouts, attend_pairs(): return lax.map(attend_one, pair_block[0])[None]  8.06 us
  transfers between devices with their start and end apart: 5, of which 3 were waited for; matrix products, arithmetic and copies ran while one was open for 15% of the time, Pallas kernels for 0%

commit v1 on v0

--- a/solution.py
+++ b/solution.py
@@ -116,11 +116,14 @@
         layer_norm(residual) * (1.0 + scale_mod[:, None, :]) + shift_mod[:, None, :]
     ).astype(jnp.bfloat16)
     columns = modulated
+
+    def cut_threads_on(body):
+        r1 = lax.axis_size("seq")
+        big = jnp.concatenate([body] * r1, axis=0)
+        return lax.all_to_all(big, axis_name="seq", split_axis=0, concat_axis=0, tiled=True)
+
     projected = jnp.einsum(
-        "tsd,dhc->thsc",
-        columns,
-        lax.all_gather(qkv_weight, "seq", axis=0, tiled=True),
-        preferred_element_type=jnp.float32,
+        "tsd,dhc->thsc", columns, cut_threads_on(qkv_weight), preferred_element_type=jnp.float32
     ).astype(jnp.bfloat16)
     pair_count = step_count * heads
     per_dev = pair_count // seq_devs

time: 331 us -> 550 us (1.66)
  waiting for transfers between devices: 137 us -> 288 us
  local copies, waits for them, and re-layouts: 27.4 us -> 73.8 us
  starting transfers between devices: 17.3 us -> 37.2 us
    all_to_all x0 -> x1, waiting for transfers between devices: none -> 221 us  [cut_threads_on(): lax.all_to_all(big, axis_name='seq', split_axis=0, concat_axis=0, tiled=T...]
    all_gather x1 -> x0, waiting for transfers between devices: 68.3 us -> none  [per_device(): lax.all_gather(qkv_weight, 'seq', axis=0, tiled=True)]
    unnamed x28 -> x67, local copies, waits for them, and re-layouts: 2.57 us -> 48 us
    all_to_all x1, starting transfers between devices: 5.48 us -> 17.3 us  [per_device(): lax.all_to_all(grouped, 'seq', split_axis=0, concat_axis=2, tiled=True)]
    all_to_all x0 -> x1, starting transfers between devices: none -> 8.77 us  [cut_threads_on(): lax.all_to_all(big, axis_name='seq', split_axis=0, concat_axis=0, tiled=T...]
  transfers between devices with their start and end apart: 5 -> 5, of which waited for: 3 -> 3; matrix products, arithmetic and copies ran while one was open for 15% -> 7% of each run, Pallas kernels for 0% -> 0%
where the time goes in v1:
time: 550 us; the launch traced here: 549 us
  waiting for transfers between devices  288 us (52%)
  blocking collectives  93 us (17%)
  local copies, waits for them, and re-layouts  73.8 us (13%)
  starting transfers between devices  37.2 us (7%)
  matrix products  34.4 us (6%)
  between operations  14.4 us (3%)
  other arithmetic  8.12 us (1%)
    all_to_all x1, waiting for transfers between devices, cut_threads_on(): lax.all_to_all(big, axis_name='seq', split_axis=0, concat_axis=0, tiled=T...  221 us
    psum x1, blocking collectives, per_device(): errors = lax.psum(partial_value, 'seq') / (tokd * seq_devs * chans)  70.3 us
    unnamed x67, local copies, waits for them, and re-layouts  48 us
    all_to_all x1, waiting for transfers between devices, per_device(): lax.all_to_all(grouped, 'seq', split_axis=0, concat_axis=2, tiled=True)  44.5 us
    all_gather x1, blocking collectives, entering(): gathered = lax.all_gather(part, axis)  22.7 us
    all_to_all x1, waiting for transfers between devices, per_device(): lax.all_to_all(routed, 'seq', split_axis=2, concat_axis=0, tiled=True)  22.2 us
    all_to_all x1, starting transfers between devices, per_device(): lax.all_to_all(grouped, 'seq', split_axis=0, concat_axis=2, tiled=True)  17.3 us
    dot_general x1, matrix products, per_device(): jnp.einsum('tsd,dhc->thsc', columns, cut_threads_on(qkv_weight), preferre...  14.6 us
  transfers between devices with their start and end apart: 5, of which 3 were waited for; matrix products, arithmetic and copies ran while one was open for 7% of the time, Pallas kernels for 0%

profile of v1, /device:TPU:1, one launch (start us, length us, event | category | flops | bytes accessed | tf_op | source)
XLA Modules:
  0.0 549.1 jit_solution(7098229690573559362)
XLA Ops:
  7.2 2.1 copy_dynamic-update-slice_fusion.30
  9.3 1.9 copy_dynamic-update-slice_fusion.29
  11.2 1.9 copy_dynamic-update-slice_fusion.28
  15.1 1.9 copy_dynamic-update-slice_fusion.26
  17.1 1.9 copy_dynamic-update-slice_fusion.25
  19.0 1.9 copy_dynamic-update-slice_fusion.24
  20.9 1.9 copy_dynamic-update-slice_fusion.23
  24.8 1.9 copy_dynamic-update-slice_fusion.21
  26.8 2.0 copy_dynamic-update-slice_fusion.20
  28.8 2.0 copy_dynamic-update-slice_fusion.19
  30.8 1.9 copy_dynamic-update-slice_fusion.18
  34.6 2.0 copy_dynamic-update-slice_fusion.16
  38.5 1.9 copy_dynamic-update-slice_fusion.14
  40.4 1.9 copy_dynamic-update-slice_fusion.13
  55.5 8.8 %all-to-all-start = ((bf16[1536,12,384]{2,1,0:T(8,128)(2,1)}), bf16[1536,12,384]{2,1,0:T(8,128)(2,1)}, u32[]{:S(2)}, u32[]{:S(2)}) async-start(bf16[1536,12,384]{2,1,0:T(8,128)(2,1)} %copy_dynamic-update-slice_fusion.31), calls=%async_computation | async-start | bytes 37748736 | tf_op jit(solution)/shard_map/all_to_all | solution.py:123
  64.3 3.7 collective-permute-start
  70.8 220.8 %all-to-all-done = bf16[1536,12,384]{2,1,0:T(8,128)(2,1)} async-done(((bf16[1536,12,384]{2,1,0:T(8,128)(2,1)}), bf16[1536,12,384]{2,1,0:T(8,128)(2,1)}, u32[]{:S(2)}, u32[]{:S(2)}) %all-to-all-start) | async-done | bytes 14155808 | tf_op jit(solution)/shard_map/all_to_all | solution.py:123
  291.6 14.6 %convert_bitcast_fusion = bf16[8,12,48,384]{3,2,0,1:T(8,128)(2,1)} fusion(bf16[1536,12,384,1]{2,1,0,3:T(8,128)(2,1)} %bitcast.9, f32[8,48,1536]{2,1,0:T(8,128)S(1)} %get-tuple-element.110, f32[8,1536]{1,0:T(8,128)S(1)} %get-tuple-element.105, f32[8,1536]{1,0:T(8,128)S(1)} %get-tuple-element.106, f32[8,48]{1,0:T(8,128)S(1)} %add_rsqrt_fusion.1, ...), kind=kOutput, calls=%fused_computation.18 | convolution fusion | flops 5440536576 | bytes 20155392 | tf_op jit(solution)/shard_map/tsd,dhc->thsc/dot_general | solution.py:125
  306.2 4.2 copy.50
  310.3 17.3 %all-to-all-start.1 = ((bf16[32,3,48,384]{3,2,1,0:T(8,128)(2,1)}), bf16[32,3,48,384]{3,2,1,0:T(8,128)(2,1)S(1)}, u32[]{:S(2)}, u32[]{:S(2)}) async-start(bf16[32,3,48,384]{3,2,1,0:T(8,128)(2,1)} %bitcast.85), calls=%async_computation.1 | async-start | bytes 7077888 | tf_op jit(solution)/shard_map/all_to_all | solution.py:131
  328.4 44.5 %all-to-all-done.1 = bf16[32,3,48,384]{3,2,1,0:T(8,128)(2,1)S(1)} async-done(((bf16[32,3,48,384]{3,2,1,0:T(8,128)(2,1)}), bf16[32,3,48,384]{3,2,1,0:T(8,128)(2,1)S(1)}, u32[]{:S(2)}, u32[]{:S(2)}) %all-to-all-start.1) | async-done | bytes 3538976 | tf_op jit(solution)/shard_map/all_to_all | solution.py:131
  373.0 2.1 copy.51
  375.1 25.9 %while.31 = (s32[]{:T(128)}, bf16[3,1536,128]{2,1,0:T(8,128)(2,1)}, bf16[3,1536,384]{2,1,0:T(8,128)(2,1)}, s32[]{:T(128)}, s32[]{:T(128)}, /*index=5*/s32[]{:T(128)}) while((s32[]{:T(128)}, bf16[3,1536,128]{2,1,0:T(8,128)(2,1)}, bf16[3,1536,384]{2,1,0:T(8,128)(2,1)}, s32[]{:T(128)}, s32[]{:T(128)}, /*index=5*/s32[]{:T(128)}) %tuple.68), condition=%wide.region_7.8_spmd, body=%wide.region_2.7_spmd.sunk | while | flops 408222720 | bytes 16001742 | solution.py:76
  376.7 6.1 %while.33 = (s32[]{:T(128)}, bf16[3,512,128]{2,1,0:T(8,128)(2,1)S(1)}, bf16[3,512,128]{2,1,0:T(8,128)(2,1)S(1)}, bf16[1536,128]{1,0:T(8,128)(2,1)S(1)}, bf16[1536,128]{1,0:T(8,128)(2,1)S(1)}, /*index=5*/s32[]{:T(128)}) while((s32[]{:T(128)}, bf16[3,512,128]{2,1,0:T(8,128)(2,1)S(1)}, bf16[3,512,128]{2,1,0:T(8,128)(2,1)S(1)}, ...), condition=%wide.region_6.6_spmd, body=%wide.region_3.5_spmd.sunk | while | flops 408222720 | bytes 10496077 | solution.py:71
  385.5 6.1 %while.33 = (s32[]{:T(128)}, bf16[3,512,128]{2,1,0:T(8,128)(2,1)S(1)}, bf16[3,512,128]{2,1,0:T(8,128)(2,1)S(1)}, bf16[1536,128]{1,0:T(8,128)(2,1)S(1)}, bf16[1536,128]{1,0:T(8,128)(2,1)S(1)}, /*index=5*/s32[]{:T(128)}) while((s32[]{:T(128)}, bf16[3,512,128]{2,1,0:T(8,128)(2,1)S(1)}, bf16[3,512,128]{2,1,0:T(8,128)(2,1)S(1)}, ...), condition=%wide.region_6.6_spmd, body=%wide.region_3.5_spmd.sunk | while | flops 408222720 | bytes 10496077 | solution.py:71
  394.1 6.1 %while.33 = (s32[]{:T(128)}, bf16[3,512,128]{2,1,0:T(8,128)(2,1)S(1)}, bf16[3,512,128]{2,1,0:T(8,128)(2,1)S(1)}, bf16[1536,128]{1,0:T(8,128)(2,1)S(1)}, bf16[1536,128]{1,0:T(8,128)(2,1)S(1)}, /*index=5*/s32[]{:T(128)}) while((s32[]{:T(128)}, bf16[3,512,128]{2,1,0:T(8,128)(2,1)S(1)}, bf16[3,512,128]{2,1,0:T(8,128)(2,1)S(1)}, ...), condition=%wide.region_6.6_spmd, body=%wide.region_3.5_spmd.sunk | while | flops 408222720 | bytes 10496077 | solution.py:71
  401.0 8.2 %copy.103 = bf16[3,1536,128]{2,0,1:T(4,128)(2,1)} copy(bf16[3,1536,128]{2,1,0:T(8,128)(2,1)} %get-tuple-element.69) | data formatting | bytes 2359296 | tf_op jit(solution)/shard_map/while | solution.py:76
  409.2 7.1 %all-to-all-start.2 = ((bf16[1,3,1536,128]{3,1,0,2:T(4,128)(2,1)}), bf16[1,3,1536,128]{3,1,0,2:T(4,128)(2,1)}, u32[]{:S(2)}, u32[]{:S(2)}) async-start(bf16[1,3,1536,128]{3,1,0,2:T(4,128)(2,1)} %bitcast.87), calls=%async_computation.2 | async-start | bytes 3145728 | tf_op jit(solution)/shard_map/all_to_all | solution.py:132
  416.5 22.2 %all-to-all-done.2 = bf16[1,3,1536,128]{3,1,0,2:T(4,128)(2,1)} async-done(((bf16[1,3,1536,128]{3,1,0,2:T(4,128)(2,1)}), bf16[1,3,1536,128]{3,1,0,2:T(4,128)(2,1)}, u32[]{:S(2)}, u32[]{:S(2)}) %all-to-all-start.2) | async-done | bytes 1179680 | tf_op jit(solution)/shard_map/all_to_all | solution.py:132
  441.4 5.5 %fusion.54 = (f32[8,48]{1,0:T(8,128)S(1)}, f32[8,48,1536]{2,1,0:T(8,128)S(1)}) fusion(f32[8,48,1536]{2,1,0:T(8,128)} %copy-done.3, bf16[1536,1536]{1,0:T(8,128)(2,1)} %all-gather.2.cloned.1.call-done, bf16[8,12,6,8,128]{4,3,2,1,0:T(8,128)(2,1)} %bitcast.89, f32[8,1536]{1,0:T(8,128)S(1)} %copy-done.14), kind=kOutput, calls=%fused_computation.109 | convolution fusion | flops 1813708416 | bytes 10667520 | tf_op jit(solution)/shard_map/tsd,de->tse/dot_general | solution.py:137
  448.0 22.7 %all_gather.7 = f32[8,48,64]{2,1,0:T(8,128)S(1)} all-gather(f32[1,48,64]{2,1,0:T(8,128)S(1)} %slice.39), channel_id=1, replica_groups=mesh['tm'=8,'seq'=32] {'tm'}, dimensions={0}, use_global_device_ids=true | all-gather | bytes 110592 | tf_op jit(solution)/shard_map/all_gather | solution.py:16
  471.5 70.3 %psum.7 = f32[8]{0:T(128)S(1)} all-reduce(f32[8]{0:T(128)S(1)} %get-tuple-element.95), channel_id=1, replica_groups=mesh['tm'=8,'seq'=32] {'seq'}, use_global_device_ids=true, to_apply=%region_14.15 | all-reduce | flops 8 | bytes 64 | tf_op jit(solution)/shard_map/psum | solution.py:155
  (125 shorter events, 55.0 us)
Async XLA Ops:
  7.2 61.0 %copy-start = (bf16[256,4608]{1,0:T(8,128)(2,1)S(1)}, bf16[256,4608]{1,0:T(8,128)(2,1)}, u32[]{:S(2)}) copy-start(bf16[256,4608]{1,0:T(8,128)(2,1)} %param.20) | copy-start | bytes 7077892
  7.2 35.2 %copy-start.2 = (bf16[48,12,384]{2,0,1:T(8,128)(2,1)S(1)}, bf16[48,12,384]{2,0,1:T(8,128)(2,1)}, u32[]{:S(2)}) copy-start(bf16[48,12,384]{2,0,1:T(8,128)(2,1)} %param.21) | copy-start | bytes 1327108
  55.5 8.8 %copy-start.6 = (f32[8,48,64]{2,1,0:T(8,128)S(1)}, f32[8,48,64]{2,1,0:T(8,128)}, u32[]{:S(2)}) copy-start(f32[8,48,64]{2,1,0:T(8,128)} %param.15) | copy-start | bytes 294916
  55.5 12.5 %copy-start.15 = (s32[8]{0:T(128)S(1)}, s32[8]{0:T(128)}, u32[]{:S(2)}) copy-start(s32[8]{0:T(128)} %param.17) | copy-start | bytes 100
  55.5 13.8 %copy-start.12 = (f32[48,64]{1,0:T(8,128)S(1)}, f32[48,64]{1,0:T(8,128)}, u32[]{:S(2)}) copy-start(f32[48,64]{1,0:T(8,128)} %param.16) | copy-start | bytes 36868
  55.5 14.4 %copy-start.11 = (bf16[64,1536]{1,0:T(8,128)(2,1)S(1)}, bf16[64,1536]{1,0:T(8,128)(2,1)}, u32[]{:S(2)}) copy-start(bf16[64,1536]{1,0:T(8,128)(2,1)} %param.19) | copy-start | bytes 589828
  55.5 236.1 %all-to-all-start = ((bf16[1536,12,384]{2,1,0:T(8,128)(2,1)}), bf16[1536,12,384]{2,1,0:T(8,128)(2,1)}, u32[]{:S(2)}, u32[]{:S(2)}) async-start(bf16[1536,12,384]{2,1,0:T(8,128)(2,1)} %copy_dynamic-update-slice_fusion.31), calls=%async_computation | async-start | bytes 37748736 | tf_op jit(solution)/shard_map/all_to_all | solution.py:123
  64.3 5.0 collective-permute-start
  69.3 236.9 %copy-start.4 = (f32[7,48,64]{2,1,0:T(8,128)}, f32[7,48,64]{2,1,0:T(8,128)S(1)}, u32[]{:S(2)}) copy-start(f32[7,48,64]{2,1,0:T(8,128)S(1)} %slice.28) | copy-start | bytes 258052
  69.3 0.6 copy-start.8
  70.4 239.9 %copy-start.3 = (f32[8,48,1536]{2,1,0:T(8,128)}, f32[8,48,1536]{2,1,0:T(8,128)S(1)}, u32[]{:S(2)}) copy-start(f32[8,48,1536]{2,1,0:T(8,128)S(1)} %get-tuple-element.110) | copy-start | bytes 7077892
  310.3 62.6 %all-to-all-start.1 = ((bf16[32,3,48,384]{3,2,1,0:T(8,128)(2,1)}), bf16[32,3,48,384]{3,2,1,0:T(8,128)(2,1)S(1)}, u32[]{:S(2)}, u32[]{:S(2)}) async-start(bf16[32,3,48,384]{3,2,1,0:T(8,128)(2,1)} %bitcast.85), calls=%async_computation.1 | async-start | bytes 7077888 | tf_op jit(solution)/shard_map/all_to_all | solution.py:131
  327.7 113.7 %all-gather.2.cloned.1.call-start = ((), (), s32[]{:S(2)}) async-start(), calls=%async_computation.3 | async-start | bytes 4866048 | tf_op jit(solution)/shard_map/all_gather | solution.py:140
  375.1 41.2 %copy-start.16 = (s32[8]{0:T(128)S(1)}, s32[8]{0:T(128)}, u32[]{:S(2)}) copy-start(s32[8]{0:T(128)} %param.17) | copy-start | bytes 100
  375.1 41.2 %copy-start.17 = (s32[8]{0:T(128)S(1)}, s32[8]{0:T(128)}, u32[]{:S(2)}) copy-start(s32[8]{0:T(128)} %param.18) | copy-start | bytes 100
  375.1 66.3 %copy-start.14 = (f32[8,1536]{1,0:T(8,128)S(1)}, f32[8,1536]{1,0:T(8,128)}, u32[]{:S(2)}) copy-start(f32[8,1536]{1,0:T(8,128)} %get-tuple-element.104) | copy-start | bytes 147460
  401.0 46.4 %copy-start.10 = (bf16[1536,64]{0,1:T(8,128)(2,1)S(1)}, bf16[1536,64]{0,1:T(8,128)(2,1)}, u32[]{:S(2)}) copy-start(bf16[1536,64]{0,1:T(8,128)(2,1)} %param.23) | copy-start | bytes 589828
  401.0 46.9 %copy-start.5 = (f32[7,48,64]{2,1,0:T(8,128)S(1)}, f32[7,48,64]{2,1,0:T(8,128)}, u32[]{:S(2)}) copy-start(f32[7,48,64]{2,1,0:T(8,128)} %copy-done.4) | copy-start | bytes 258052
  401.0 46.9 %copy-start.9 = (f32[1,48,64]{2,1,0:T(8,128)S(1)}, f32[1,48,64]{2,1,0:T(8,128)}, u32[]{:S(2)}) copy-start(f32[1,48,64]{2,1,0:T(8,128)} %copy-done.8) | copy-start | bytes 36868
  401.0 69.7 %copy-start.13 = (f32[48,64]{1,0:T(8,128)S(1)}, f32[48,64]{1,0:T(8,128)}, u32[]{:S(2)}) copy-start(f32[48,64]{1,0:T(8,128)} %param.16) | copy-start | bytes 36868
  401.0 69.8 %copy-start.7 = (f32[8,48,64]{2,1,0:T(8,128)S(1)}, f32[8,48,64]{2,1,0:T(8,128)}, u32[]{:S(2)}) copy-start(f32[8,48,64]{2,1,0:T(8,128)} %param.15) | copy-start | bytes 294916
  401.0 141.3 %copy-start.1 = (bf16[256,4608]{1,0:T(8,128)(2,1)S(1)}, bf16[256,4608]{1,0:T(8,128)(2,1)}, u32[]{:S(2)}) copy-start(bf16[256,4608]{1,0:T(8,128)(2,1)} %param.20) | copy-start | bytes 7077892
  409.2 29.5 %all-to-all-start.2 = ((bf16[1,3,1536,128]{3,1,0,2:T(4,128)(2,1)}), bf16[1,3,1536,128]{3,1,0,2:T(4,128)(2,1)}, u32[]{:S(2)}, u32[]{:S(2)}) async-start(bf16[1,3,1536,128]{3,1,0,2:T(4,128)(2,1)} %bitcast.87), calls=%async_computation.2 | async-start | bytes 3145728 | tf_op jit(solution)/shard_map/all_to_all | solution.py:132
Sparse Core Ops, SparseCore 0:
  331.0 70.2 all-gather.1
